TPU v7x, 32 devices: a whole 2x2x4 slice. The times are simulated.
32 devices in a mesh: depth: 2 (over y), lat: 8 (over z, x), freq: 2 (over core).
Axes of the slice: x: 2, y: 2, z: 4, core: 2. Of those that a mesh axis runs over, the one named last changes fastest.
Arguments:
- surface: bfloat16 [6, 2, 128, 8192], P('freq', None, None, 'lat'), may hold values from -6 to 6
- refl: float32 [2, 8192], P('depth', 'lat'), may hold values from -0.5 to 0.5
- pool: bfloat16 [2, 6, 8, 128, 256], P('depth', 'freq'), may hold values from -0.375 to 0.375
- tile_ids: int32 [2, 64, 10], P('depth', 'lat'), may hold values from 0 to 63, as said below
- block_ids: int32 [2, 64, 10], P('depth', 'lat'), may hold values from 0 to 7
- counts: int32 [2, 64], P('depth', 'lat'), may hold values from 1 to 10, as said below
Outputs:
- image: float32 [2, 8192], P('depth', 'lat')
Inputs may be any that keep to these rules, and one draw needn't show every extreme that they name: tile_ids[l, j, k] = (j + o) mod 64 for an offset o with -8 <= o <= 8; slot 0 names the row's own tile; in every level some row has all 10 slots live with offsets 8 at slot 1 and -8 at slot 2. Slots k >= counts[l, j] of row j are padding; in every level some row has all 10 slots live.
All inputs are finite; a program needn't handle non-finite values.
Results may differ from a plain program's by a relative error of at most 0.00055.
Values may be sent and summed in bfloat16 or wider, within the bound.
No kernel may reach another device: no remote copies, remote signals or barrier semaphores. Data moves between devices by JAX's collectives and lax.ppermute only.
A program may use at most 128 MiB of HBM per device.

v0:
```python
import jax
import jax.numpy as jnp
from jax import lax
from jax.sharding import PartitionSpec as P

TILE = 128
TILE_DEV = 8


def extended_2(block, sides, width):
    for axis, dim in sides:
        count = lax.axis_size(axis)
        forward = [(i, i + 1) for i in range(count - 1)]
        forward.append((count - 1, 0))
        backward = [(target, source) for source, target in forward]
        low = lax.ppermute(
            lax.slice_in_dim(block, block.shape[dim] - width, None, axis=dim), axis, forward
        )
        high = lax.ppermute(lax.slice_in_dim(block, 0, width, axis=dim), axis, backward)
        block = jnp.concatenate([low, block, high], axis=dim)
    return block


def aperture_rim(wave_field):
    return extended_2(wave_field, (("lat", 3),), TILE_DEV * TILE)


def extrapolate(extended, pool_level, local_ids, block_level, count_level, refl_level):
    freqs_here = extended.shape[0]
    shot_rows = extended.shape[2]
    tile_rows = local_ids.shape[0]
    slot_total = local_ids.shape[1]
    tile_grid = extended.reshape(freqs_here, 2, shot_rows, -1, TILE)
    slot_live = (jnp.arange(slot_total)[None, :] < count_level[:, None]).astype(jnp.bfloat16)
    picked = jnp.take(tile_grid, local_ids, axis=3) * slot_live[None, None, None, :, :, None]
    chosen = jnp.take(pool_level, block_level, axis=1)
    product = jnp.einsum("fsarkt,frktc->rfsac", picked, chosen, preferred_element_type=jnp.float32)
    real_part = product[:, :, 0, :, :TILE] - product[:, :, 1, :, TILE:]
    imag_part = product[:, :, 0, :, TILE:] + product[:, :, 1, :, :TILE]
    row_scale = 1.0 / jnp.sqrt(count_level.astype(jnp.float32))
    rows_out = jnp.stack([real_part, imag_part], 2) * row_scale[:, None, None, None, None]
    wave_out = jnp.transpose(rows_out, (1, 2, 3, 0, 4)).reshape(
        freqs_here, 2, shot_rows, tile_rows * TILE
    )
    wave_out = wave_out * (1.0 - refl_level)
    return (wave_out.astype(jnp.bfloat16), jnp.sum(wave_out * wave_out, axis=(0, 1, 2)))


def per_device(surface, refl, pool, tile_ids, block_ids, counts):
    depth_index = lax.axis_index("depth")
    lat_index = lax.axis_index("lat")
    tile_count = TILE_DEV * lax.axis_size("lat")
    first_tile = lat_index * TILE_DEV - TILE_DEV
    freqs_here = surface.shape[0]
    shot_total = surface.shape[2]
    lateral_width = surface.shape[3]
    shot_rows = shot_total // lax.axis_size("depth")
    own_shots = lax.dynamic_slice_in_dim(surface, depth_index * shot_rows, shot_rows, 2)
    pool_all = lax.all_gather(pool, "depth", axis=0, tiled=True)
    ids_all, blocks_all, counts_all = (
        lax.all_gather(tile_ids, "depth", axis=0, tiled=True),
        lax.all_gather(block_ids, "depth", axis=0, tiled=True),
        lax.all_gather(counts, "depth", axis=0, tiled=True),
    )
    refl_all = lax.all_gather(refl, "depth", axis=0, tiled=True)
    level_total = pool_all.shape[0]

    def level_step(level_index, loop_state):
        wave_field, images = loop_state
        ids_here = lax.dynamic_index_in_dim(ids_all, level_index, 0, keepdims=False)
        local_level = jnp.mod(ids_here - first_tile, tile_count)
        pool_here = lax.dynamic_index_in_dim(pool_all, level_index, 0, keepdims=False)
        blocks_here = lax.dynamic_index_in_dim(blocks_all, level_index, 0, keepdims=False)
        counts_here = lax.dynamic_index_in_dim(counts_all, level_index, 0, keepdims=False)
        refl_here = lax.dynamic_index_in_dim(refl_all, level_index, 0, keepdims=False)
        handed, partial_value = extrapolate(
            aperture_rim(wave_field), pool_here, local_level, blocks_here, counts_here, refl_here
        )
        images = lax.dynamic_update_index_in_dim(images, partial_value, level_index, 0)
        return (handed, images)

    start_images = jnp.zeros((level_total, lateral_width), jnp.float32)
    loop_state = lax.fori_loop(0, level_total, level_step, (own_shots, start_images))
    image_local = lax.psum_scatter(loop_state[1], "depth", scatter_dimension=0, tiled=True)[0]
    summed = lax.psum(image_local, "freq")
    divisor = freqs_here * lax.axis_size("freq") * shot_total
    return (summed / divisor)[None, :]


def solution(mesh):
    placed = (
        P("freq", None, None, "lat"),
        P("depth", "lat"),
        P("depth", "freq", None, None, None),
        P("depth", "lat", None),
        P("depth", "lat", None),
        P("depth", "lat"),
    )
    return jax.shard_map(
        per_device, mesh=mesh, in_specs=placed, out_specs=P("depth", "lat"), check_vma=False
    )
```

profile of v0, /device:TPU:0, one launch (start us, length us, event | category | flops | bytes accessed | tf_op | source)
XLA Modules:
  0.0 194.0 jit_solution(9081155011961694617)
XLA Ops:
  6.5 0.7 all-gather.4.cloned.1.call-update
  7.3 5.4 %all-gather = s32[2,1,8]{2,1,0:T(1,128)S(1)} all-gather(s32[1,1,8]{2,1,0:T(1,128)} %bitcast.109), channel_id=1, replica_groups=mesh['depth'=2,'lat'=8,'freq'=2] {'depth'}, dimensions={0}, use_global_device_ids=true | all-gather | bytes 96 | tf_op jit(solution)/shard_map/all_gather | solution.py:63
  12.7 4.5 %all-gather.1 = f32[2,1,1024]{2,1,0:T(1,128)S(1)} all-gather(f32[1,1,1024]{2,1,0:T(1,128)} %bitcast.108), channel_id=1, replica_groups=mesh['depth'=2,'lat'=8,'freq'=2] {'depth'}, dimensions={0}, use_global_device_ids=true | all-gather | bytes 12288 | tf_op jit(solution)/shard_map/all_gather | solution.py:65
  17.2 1.2 dynamic-slice
  18.4 4.5 %all_gather.15 = s32[2,8,10]{2,1,0:T(8,128)S(1)} all-gather(s32[1,8,10]{2,1,0:T(8,128)} %param.11), channel_id=1, replica_groups=mesh['depth'=2,'lat'=8,'freq'=2] {'depth'}, dimensions={0}, use_global_device_ids=true | all-gather | bytes 960 | tf_op jit(solution)/shard_map/all_gather | solution.py:61
  22.9 4.8 %all_gather.17 = s32[2,8,10]{2,1,0:T(8,128)S(1)} all-gather(s32[1,8,10]{2,1,0:T(8,128)} %param.12), channel_id=1, replica_groups=mesh['depth'=2,'lat'=8,'freq'=2] {'depth'}, dimensions={0}, use_global_device_ids=true | all-gather | bytes 960 | tf_op jit(solution)/shard_map/all_gather | solution.py:62
  27.7 1.0 constant_dynamic-slice_fusion.2
  28.7 28.0 %all-gather.4.cloned.1.call-done = bf16[2,3,8,128,256]{4,3,2,1,0:T(8,128)(2,1)} async-done(((bf16[1,3,8,128,256]{4,3,2,1,0:T(8,128)(2,1)}), bf16[2,3,8,128,256]{4,3,2,1,0:T(8,128)(2,1)}) %all-gather.4.cloned.1.call-update) | async-done | bytes 3145744 | tf_op jit(solution)/shard_map/all_gather | solution.py:59
  56.7 121.8 %while.17 = (s32[]{:T(128)}, bf16[3,2,64,1024]{3,2,1,0:T(8,128)(2,1)}, f32[2,1024]{1,0:T(2,128)S(1)}, s32[2,8,10]{2,1,0:T(8,128)S(1)}, s32[]{:T(128)}, /*index=5...) while((s32[]{:T(128)}, ...), condition=%wide.region_2.3_spmd, body=%wide.region_0.2_spmd.sunk | while | flops 2040010240 | bytes 96773536 | solution.py:83
  56.7 4.2 %collective-permute-start = (bf16[3,2,64,1024]{3,2,1,0:T(8,128)(2,1)}, bf16[3,2,64,1024]{3,2,1,0:T(8,128)(2,1)}, u32[]{:S(2)}, u32[]{:S(2)}) collective-permute-start(bf16[3,2,64,1024]{3,2,1,0:T(8,128)(2,1)} %get-tuple-element.336), channel_id=1, source_target_pairs={{2,0},{4,2},{6,4},{8,6},{10,8},{12,10},{14,12},{0,14},{3,1},{5,3},... | collective-permute-start | bytes 2359304 | tf_op jit(solution)/shard_map/while/body/eval_jaxpr/ppermute | solution.py:19
  60.9 1.5 dynamic-slice_bitcast_fusion.2
  62.6 8.1 %gather_fusion = bf16[80,3,128,256]{3,2,1,0:T(8,128)(2,1)} fusion(bf16[3,8,128,256]{3,2,1,0:T(8,128)(2,1)S(1)} %dynamic-slice_bitcast_fusion.2, s32[1024]{0:T(1024)S(1)} %pad_clamp_fusion.4), kind=kCustom, calls=%fused_computation.1.clone.1 | custom fusion | bytes 31457600 | tf_op jit(solution)/shard_map/while/body/eval_jaxpr/jit(_take)/gather | solution.py:36
  70.9 22.2 %collective-permute-done = bf16[3,2,64,1024]{3,2,1,0:T(8,128)(2,1)} collective-permute-done((bf16[3,2,64,1024]{3,2,1,0:T(8,128)(2,1)}, bf16[3,2,64,1024]{3,2,1,0:T(8,128)(2,1)}, u32[]{:S(2)}, u32[]{:S(2)}) %collective-permute-start) | collective-permute-done | bytes 786464 | tf_op jit(solution)/shard_map/while/body/eval_jaxpr/ppermute | solution.py:19
  93.1 3.6 %copy_bitcast_fusion.3 = bf16[3,2,64,24,128]{4,2,3,1,0:T(8,128)(2,1)} fusion(bf16[3,2,64,1024]{3,2,1,0:T(8,128)(2,1)} %collective-permute-done, bf16[3,2,64,1024]{3,2,1,0:T(8,128)(2,1)} %get-tuple-element.336, bf16[3,2,64,1024]{3,2,1,0:T(8,128)(2,1)} %collective-permute-done.1), kind=kLoop, calls=%fused_computation.7.clone.1 | loop fusion | flops 7077888 | bytes 4718592 | tf_op jit(solution)/shard_map/while/body/eval_jaxpr/reshape | solution.py:33
  96.7 8.5 %gather_fusion.1 = bf16[80,3,2,64,128]{4,3,2,1,0:T(8,128)(2,1)} fusion(bf16[3,2,64,24,128]{4,2,3,1,0:T(8,128)(2,1)} %copy_bitcast_fusion.3, s32[1024]{0:T(1024)S(1)} %pad_clamp_fusion.5), kind=kCustom, calls=%fused_computation.clone.1 | custom fusion | bytes 15728960 | tf_op jit(solution)/shard_map/while/body/eval_jaxpr/jit(_take)/gather | solution.py:35
  105.2 10.2 %fusion.29 = f32[8,3,2,64,256]{4,3,2,1,0:T(8,128)S(1)} fusion(bf16[8,10,3,128,256]{4,3,2,1,0:T(8,128)(2,1)} %bitcast.101, pred[8,10]{1,0:T(8,128)(4,1)S(1)} %get-tuple-element.317, bf16[8,10,3,2,64,128]{5,4,3,2,1,0:T(8,128)(2,1)} %bitcast.100, pred[8,10]{1,0:T(8,128)(4,1)S(1)} %get-tuple-element.319, bf16[8,10]{1,0:T(8,128)(2,1)S(1)} %fusion.28), kind=kOutput, calls=%fused_computation.9.clone.1 | convolution fusion | flops 2028994560 | bytes 26739008 | tf_op jit(solution)/shard_map/while/body/eval_jaxpr/fsarkt,frktc->rfsac/dot_general | solution.py:37
  115.5 0.2 slice_subtract_fusion.2
  115.7 0.3 fusion.31
  116.0 1.2 fusion.30
  117.2 4.5 %collective-permute-start = (bf16[3,2,64,1024]{3,2,1,0:T(8,128)(2,1)}, bf16[3,2,64,1024]{3,2,1,0:T(8,128)(2,1)}, u32[]{:S(2)}, u32[]{:S(2)}) collective-permute-start(bf16[3,2,64,1024]{3,2,1,0:T(8,128)(2,1)} %get-tuple-element.336), channel_id=1, source_target_pairs={{2,0},{4,2},{6,4},{8,6},{10,8},{12,10},{14,12},{0,14},{3,1},{5,3},... | collective-permute-start | bytes 2359304 | tf_op jit(solution)/shard_map/while/body/eval_jaxpr/ppermute | solution.py:19
  121.7 1.5 dynamic-slice_bitcast_fusion.2
  123.4 8.2 %gather_fusion = bf16[80,3,128,256]{3,2,1,0:T(8,128)(2,1)} fusion(bf16[3,8,128,256]{3,2,1,0:T(8,128)(2,1)S(1)} %dynamic-slice_bitcast_fusion.2, s32[1024]{0:T(1024)S(1)} %pad_clamp_fusion.4), kind=kCustom, calls=%fused_computation.1.clone.1 | custom fusion | bytes 31457600 | tf_op jit(solution)/shard_map/while/body/eval_jaxpr/jit(_take)/gather | solution.py:36
  131.7 22.7 %collective-permute-done = bf16[3,2,64,1024]{3,2,1,0:T(8,128)(2,1)} collective-permute-done((bf16[3,2,64,1024]{3,2,1,0:T(8,128)(2,1)}, bf16[3,2,64,1024]{3,2,1,0:T(8,128)(2,1)}, u32[]{:S(2)}, u32[]{:S(2)}) %collective-permute-start) | collective-permute-done | bytes 786464 | tf_op jit(solution)/shard_map/while/body/eval_jaxpr/ppermute | solution.py:19
  154.4 3.6 %copy_bitcast_fusion.3 = bf16[3,2,64,24,128]{4,2,3,1,0:T(8,128)(2,1)} fusion(bf16[3,2,64,1024]{3,2,1,0:T(8,128)(2,1)} %collective-permute-done, bf16[3,2,64,1024]{3,2,1,0:T(8,128)(2,1)} %get-tuple-element.336, bf16[3,2,64,1024]{3,2,1,0:T(8,128)(2,1)} %collective-permute-done.1), kind=kLoop, calls=%fused_computation.7.clone.1 | loop fusion | flops 7077888 | bytes 4718592 | tf_op jit(solution)/shard_map/while/body/eval_jaxpr/reshape | solution.py:33
  158.0 8.5 %gather_fusion.1 = bf16[80,3,2,64,128]{4,3,2,1,0:T(8,128)(2,1)} fusion(bf16[3,2,64,24,128]{4,2,3,1,0:T(8,128)(2,1)} %copy_bitcast_fusion.3, s32[1024]{0:T(1024)S(1)} %pad_clamp_fusion.5), kind=kCustom, calls=%fused_computation.clone.1 | custom fusion | bytes 15728960 | tf_op jit(solution)/shard_map/while/body/eval_jaxpr/jit(_take)/gather | solution.py:35
  166.6 10.2 %fusion.29 = f32[8,3,2,64,256]{4,3,2,1,0:T(8,128)S(1)} fusion(bf16[8,10,3,128,256]{4,3,2,1,0:T(8,128)(2,1)} %bitcast.101, pred[8,10]{1,0:T(8,128)(4,1)S(1)} %get-tuple-element.317, bf16[8,10,3,2,64,128]{5,4,3,2,1,0:T(8,128)(2,1)} %bitcast.100, pred[8,10]{1,0:T(8,128)(4,1)S(1)} %get-tuple-element.319, bf16[8,10]{1,0:T(8,128)(2,1)S(1)} %fusion.28), kind=kOutput, calls=%fused_computation.9.clone.1 | convolution fusion | flops 2028994560 | bytes 26739008 | tf_op jit(solution)/shard_map/while/body/eval_jaxpr/fsarkt,frktc->rfsac/dot_general | solution.py:37
  177.0 0.3 fusion.31
  177.3 1.2 fusion.30
  178.5 5.0 %all-reduce = f32[2,1024]{1,0:T(2,128)S(1)} all-reduce(f32[2,1024]{1,0:T(2,128)S(1)} %get-tuple-element.226), channel_id=2, replica_groups=mesh['depth'=2,'lat'=8,'freq'=2] {'depth'}, use_global_device_ids=true, to_apply=%region_3.4.clone | all-reduce | flops 2048 | bytes 16384
  183.5 0.6 constant_dynamic-slice_fusion.1
  184.1 2.5 %psum.7 = f32[1024]{0:T(1024)S(1)} all-reduce(f32[1024]{0:T(1024)S(1)} %bitcast.106), channel_id=1, replica_groups=mesh['depth'=2,'lat'=8,'freq'=2] {'freq'}, use_global_device_ids=true, to_apply=%region_4.5 | all-reduce | flops 1024 | bytes 8192 | tf_op jit(solution)/shard_map/psum | solution.py:85
  186.6 0.6 broadcast_multiply_fusion
  (30 shorter events, 0.9 us)
Async XLA Ops:
  6.5 21.1 %copy-start = (bf16[3,2,128,1024]{3,2,1,0:T(8,128)(2,1)S(1)}, bf16[3,2,128,1024]{3,2,1,0:T(8,128)(2,1)}, u32[]{:S(2)}) copy-start(bf16[3,2,128,1024]{3,2,1,0:T(8,128)(2,1)} %param.8) | copy-start | bytes 4718596
  6.5 50.1 %all-gather.4.cloned.1.call-start = ((), (), s32[]{:S(2)}) async-start(), calls=%async_computation | async-start | bytes 4718592 | tf_op jit(solution)/shard_map/all_gather | solution.py:59
  56.7 36.4 %collective-permute-start = (bf16[3,2,64,1024]{3,2,1,0:T(8,128)(2,1)}, bf16[3,2,64,1024]{3,2,1,0:T(8,128)(2,1)}, u32[]{:S(2)}, u32[]{:S(2)}) collective-permute-start(bf16[3,2,64,1024]{3,2,1,0:T(8,128)(2,1)} %get-tuple-element.336), channel_id=1, source_target_pairs={{2,0},{4,2},{6,4},{8,6},{10,8},{12,10},{14,12},{0,14},{3,1},{5,3},... | collective-permute-start | bytes 2359304 | tf_op jit(solution)/shard_map/while/body/eval_jaxpr/ppermute | solution.py:19
  60.9 32.1 %collective-permute-start.1 = (bf16[3,2,64,1024]{3,2,1,0:T(8,128)(2,1)}, bf16[3,2,64,1024]{3,2,1,0:T(8,128)(2,1)}, u32[]{:S(2)}, u32[]{:S(2)}) collective-permute-start(bf16[3,2,64,1024]{3,2,1,0:T(8,128)(2,1)} %get-tuple-element.336), channel_id=1, source_target_pairs={{0,2},{2,4},{4,6},{6,8},{8,10},{10,12},{12,14},{14,0},{1,3},{3,5},... | collective-permute-start | bytes 2359304 | tf_op jit(solution)/shard_map/while/body/eval_jaxpr/ppermute | solution.py:16
  117.2 37.2 %collective-permute-start = (bf16[3,2,64,1024]{3,2,1,0:T(8,128)(2,1)}, bf16[3,2,64,1024]{3,2,1,0:T(8,128)(2,1)}, u32[]{:S(2)}, u32[]{:S(2)}) collective-permute-start(bf16[3,2,64,1024]{3,2,1,0:T(8,128)(2,1)} %get-tuple-element.336), channel_id=1, source_target_pairs={{2,0},{4,2},{6,4},{8,6},{10,8},{12,10},{14,12},{0,14},{3,1},{5,3},... | collective-permute-start | bytes 2359304 | tf_op jit(solution)/shard_map/while/body/eval_jaxpr/ppermute | solution.py:19
  121.7 32.8 %collective-permute-start.1 = (bf16[3,2,64,1024]{3,2,1,0:T(8,128)(2,1)}, bf16[3,2,64,1024]{3,2,1,0:T(8,128)(2,1)}, u32[]{:S(2)}, u32[]{:S(2)}) collective-permute-start(bf16[3,2,64,1024]{3,2,1,0:T(8,128)(2,1)} %get-tuple-element.336), channel_id=1, source_target_pairs={{0,2},{2,4},{4,6},{6,8},{8,10},{10,12},{12,14},{14,0},{1,3},{3,5},... | collective-permute-start | bytes 2359304 | tf_op jit(solution)/shard_map/while/body/eval_jaxpr/ppermute | solution.py:16
Sparse Core Ops, SparseCore 0:
  8.9 47.7 all-gather.3
where the time goes:
time: 194 us
  waiting for transfers between devices  73.6 us (38%)
  local copies, waits for them, and re-layouts  39.5 us (20%)
  blocking collectives  26.7 us (14%)
  matrix products  20.5 us (11%)
  between operations  13.4 us (7%)
  other arithmetic  11.5 us (6%)
  starting transfers between devices  8.71 us (4%)
    ppermute x2, waiting for transfers between devices, extended_2(): lax.ppermute(lax.slice_in_dim(block, 0, width, axis=dim), axis, backward)  44.9 us
    all_gather x1, waiting for transfers between devices, per_device(): pool_all = lax.all_gather(pool, 'depth', axis=0, tiled=True)  28 us
    dot_general x2, matrix products, extrapolate(): jnp.einsum('fsarkt,frktc->rfsac', picked, chosen, preferred_element_type=...  20.5 us
    gather x2, local copies, waits for them, and re-layouts, extrapolate(): jnp.take(tile_grid, local_ids, axis=3)  17 us
    gather x2, local copies, waits for them, and re-layouts, extrapolate(): chosen = jnp.take(pool_level, block_level, axis=1)  16.3 us
    ppermute x2, starting transfers between devices, extended_2(): lax.ppermute(lax.slice_in_dim(block, 0, width, axis=dim), axis, backward)  8.71 us
    reshape x2, other arithmetic, extrapolate(): tile_grid = extended.reshape(freqs_here, 2, shot_rows, -1, TILE)  7.29 us
    all_gather x1, blocking collectives, per_device(): lax.all_gather(counts, 'depth', axis=0, tiled=True)  5.4 us
  transfers between devices with their start and end apart: 5, of which 3 were waited for; matrix products, arithmetic and copies ran while one was open for 11% of the time, Pallas kernels for 0%

commit v1 on v0

--- a/solution.py
+++ b/solution.py
@@ -1,6 +1,10 @@
+import functools
+
 import jax
 import jax.numpy as jnp
 from jax import lax
+from jax.experimental import pallas as pl
+from jax.experimental.pallas import tpu as pltpu
 from jax.sharding import PartitionSpec as P
 
 TILE = 128
@@ -87,6 +91,255 @@
     return (summed / divisor)[None, :]
 
 
+HALF = TILE // 2
+VMEM_SPACE = pl.BlockSpec(memory_space=pltpu.VMEM)
+ANY_SPACE = pl.BlockSpec(memory_space=pl.ANY)
+
+
+def pack_kernel(lat_size, depth_ref, surface_ref, tables_ref, out_ref, own_buf, half_buf, sems):
+    depth_index = depth_ref[0]
+    half_shots = half_buf.shape[1]
+    shots_own = own_buf.shape[1] // lat_size
+    shots_half = half_shots // lat_size
+    tiles = own_buf.shape[2] // TILE
+    own_copy = pltpu.make_async_copy(surface_ref.at[2 * depth_index], own_buf, sems.at[0])
+    half_copy = pltpu.make_async_copy(
+        surface_ref.at[1, :, pl.ds(depth_index * half_shots, half_shots), :], half_buf, sems.at[1]
+    )
+    own_copy.start()
+    half_copy.start()
+    base_half = tiles * shots_own
+    base_table = base_half + tiles * shots_half
+    refl = tables_ref[0, :tiles, :]
+    high = refl.astype(jnp.bfloat16).astype(jnp.float32)
+    rest = refl - high
+    middle = rest.astype(jnp.bfloat16).astype(jnp.float32)
+    low = rest - middle
+    lists = tables_ref[0, tiles:, :] + pltpu.roll(tables_ref[1, tiles:, :], HALF, 1)
+    rows_left = jnp.concatenate([high, low], axis=0).astype(jnp.bfloat16)
+    rows_right = jnp.concatenate([middle, lists], axis=0).astype(jnp.bfloat16)
+    for target in range(lat_size):
+        out_ref[target, base_table:, :TILE] = rows_left
+        out_ref[target, base_table:, TILE:] = rows_right
+    own_copy.wait()
+    for target in range(lat_size):
+        for part in range(2):
+            for tile in range(tiles):
+                out_ref[
+                    target, tile * shots_own:(tile + 1) * shots_own, part * TILE:(part + 1) * TILE
+                ] = own_buf[
+                    part, target * shots_own:(target + 1) * shots_own, tile * TILE:(tile + 1) * TILE
+                ]
+    half_copy.wait()
+    for pair in range(lat_size // 2):
+        for part in range(2):
+            for tile in range(0, tiles, 2):
+                rows = slice(pair * 2 * shots_half, (pair + 1) * 2 * shots_half)
+                even = half_buf[part, rows, tile * TILE:(tile + 1) * TILE].astype(jnp.float32)
+                odd = half_buf[part, rows, (tile + 1) * TILE:(tile + 2) * TILE].astype(jnp.float32)
+                start = base_half + tile * shots_half
+                lanes = slice(part * TILE, (part + 1) * TILE)
+                for side in range(2):
+                    part_rows = slice(side * shots_half, (side + 1) * shots_half)
+                    joined = jnp.concatenate([even[part_rows], odd[part_rows]], axis=0)
+                    out_ref[2 * pair + side, start:start + 2 * shots_half, lanes] = joined.astype(
+                        jnp.bfloat16
+                    )
+
+
+def level_kernel(
+    shots, row_start, levels, slots, index_ref, scale_ref, wave_ref, local_ref, remote_ref,
+    image_in_ref, depth_ref, freq_ref, image_ref, pool_buf, table, wave_buf, pass_buf, sems,
+):
+    lat_size = wave_ref.shape[0]
+    blocks = pool_buf.shape[1]
+    tiles = table.shape[0] - 1
+    entries = tiles // blocks
+    per_source = entries // lat_size
+    depth_index = depth_ref[0]
+    freq_index = freq_ref[0]
+    copies = [
+        pltpu.make_async_copy(local_ref.at[0, freq_index], pool_buf.at[depth_index], sems.at[0]),
+        pltpu.make_async_copy(remote_ref, pool_buf.at[1 - depth_index], sems.at[1]),
+    ]
+    for copy in copies:
+        copy.start()
+    rows_source = per_source * shots
+    row_table = per_source * 24
+    for source in range(lat_size):
+        refl = (
+            wave_ref[source, row_table:row_table + per_source, :TILE].astype(jnp.float32)
+            + wave_ref[source, row_table:row_table + per_source, TILE:].astype(jnp.float32)
+        ) + wave_ref[source, row_table + per_source:row_table + 2 * per_source, :TILE].astype(
+            jnp.float32
+        )
+        pass_buf[source * per_source:(source + 1) * per_source, :] = 1.0 - refl
+    table[tiles] = jnp.zeros(table.shape[1:], table.dtype)
+    for copy in copies:
+        copy.wait()
+    sources_step = lat_size // 2
+
+    for level in range(levels):
+        last = level == levels - 1
+
+        def block_step(block, carry):
+            upper = pool_buf[level, block]
+            lower = jnp.concatenate([-upper[:, TILE:], upper[:, :TILE]], axis=1)
+            weights = jnp.concatenate([upper, lower], axis=0)
+            for step in range(2):
+                if level == 0:
+                    left = wave_ref[
+                        step * sources_step:(step + 1) * sources_step,
+                        row_start:row_start + rows_source, :
+                    ].reshape(sources_step * rows_source, 2 * TILE)
+                else:
+                    left = wave_buf[
+                        step * sources_step * rows_source:(step + 1) * sources_step * rows_source, :
+                    ]
+                product = jnp.dot(left, weights, preferred_element_type=jnp.float32)
+                count = sources_step * per_source
+                table[pl.ds(block * entries + step * count, count)] = product.reshape(
+                    count, shots, 2 * TILE
+                )
+            return carry
+
+        lax.fori_loop(0, blocks, block_step, 0)
+        rows_step = max(1, 16 // shots)
+
+        def row_step(step, carry):
+            outs = []
+            for inner in range(rows_step):
+                row = step * rows_step + inner
+                base = (level * entries + row) * slots
+                total = table[index_ref[base]]
+                for slot in range(1, slots):
+                    total = total + table[index_ref[base + slot]]
+                total = total * scale_ref[level * entries + row]
+                if not last:
+                    kept = pass_buf[pl.ds(row, 1), :]
+                    total = total * jnp.concatenate([kept, kept], axis=1)
+                    outs.append(total)
+                squares = total * total
+                squares = squares[:, :TILE] + squares[:, TILE:]
+                line = jnp.sum(squares, axis=0, keepdims=True)
+                image_ref[pl.ds(level * entries + row, 1), :] = (
+                    image_in_ref[pl.ds(level * entries + row, 1), :] + line
+                )
+            if not last:
+                joined = jnp.concatenate(outs, axis=0) if rows_step > 1 else outs[0]
+                height = rows_step * shots
+                start = pl.multiple_of(step * height, height)
+                wave_buf[pl.ds(start, height), :] = joined.astype(jnp.bfloat16)
+            return carry
+
+        lax.fori_loop(0, entries // rows_step, row_step, 0)
+
+
+def run_levels(shots, row_start, index, scale, wave, local, remote, image, depth_id, freq_id):
+    blocks = local.shape[2]
+    levels = scale.shape[0]
+    entries = scale.shape[1]
+    slots = index.size // scale.size
+    smem = pl.BlockSpec(memory_space=pltpu.SMEM)
+    return pl.pallas_call(
+        functools.partial(level_kernel, shots, row_start, levels, slots),
+        out_shape=jax.ShapeDtypeStruct((levels * entries, TILE), jnp.float32),
+        in_specs=[smem, smem, VMEM_SPACE, ANY_SPACE, ANY_SPACE, VMEM_SPACE, smem, smem],
+        out_specs=VMEM_SPACE,
+        scratch_shapes=[
+            pltpu.VMEM((levels, blocks, TILE, 2 * TILE), jnp.bfloat16),
+            pltpu.VMEM((blocks * entries + 1, shots, 2 * TILE), jnp.float32),
+            pltpu.VMEM((entries * shots, 2 * TILE), jnp.bfloat16),
+            pltpu.VMEM((entries, TILE), jnp.float32),
+            pltpu.SemaphoreType.DMA((2,)),
+        ],
+        cost_estimate=pl.CostEstimate(
+            flops=2 * levels * blocks * entries * shots * 4 * TILE * TILE,
+            bytes_accessed=8 * entries * shots * TILE + 8 * blocks * TILE * TILE,
+            transcendentals=0,
+        ),
+        name="levels_" + str(shots),
+    )(index.reshape(-1), scale.reshape(-1), wave, local, remote, image, depth_id, freq_id)
+
+
+def per_device_fast(surface, refl, pool, tile_ids, block_ids, counts):
+    depth_index = lax.axis_index("depth")
+    depth_size = lax.axis_size("depth")
+    lat_size = lax.axis_size("lat")
+    freqs_here, _, shot_total, lateral_width = surface.shape
+    tile_rows, slots = tile_ids.shape[1:]
+    blocks = pool.shape[2]
+    levels = depth_size
+    entries = tile_rows * lat_size
+    shots_own = shot_total // lat_size
+    shots_half = shots_own // 2
+    swap = [(0, 1), (1, 0)]
+    theirs = lax.dynamic_index_in_dim(pool[0], 2 * (1 - depth_index), 0, keepdims=False)
+    remote_own = lax.ppermute(theirs, "depth", swap)
+    remote_half = lax.ppermute(pool[0, 1], "depth", swap)
+    lists = jnp.concatenate([tile_ids[0], block_ids[0], counts[0][:, None]], axis=1).astype(jnp.float32)
+    lists = jnp.pad(lists, ((0, 0), (0, TILE - lists.shape[1])))
+    tables = jnp.concatenate([refl.reshape(tile_rows, TILE), lists], axis=0)[None]
+    tables = lax.all_gather(tables, "depth", axis=0, tiled=True)
+    depth_id = depth_index.astype(jnp.int32).reshape(1)
+    rows = tile_rows * (shots_own + shots_half + 2)
+    packed = pl.pallas_call(
+        functools.partial(pack_kernel, lat_size),
+        out_shape=jax.ShapeDtypeStruct((lat_size, rows, 2 * TILE), jnp.bfloat16),
+        in_specs=[pl.BlockSpec(memory_space=pltpu.SMEM), ANY_SPACE, VMEM_SPACE],
+        out_specs=VMEM_SPACE,
+        scratch_shapes=[
+            pltpu.VMEM((2, shot_total, lateral_width), jnp.bfloat16),
+            pltpu.VMEM((2, shot_total // 2, lateral_width), jnp.bfloat16),
+            pltpu.SemaphoreType.DMA((2,)),
+        ],
+        name="pack",
+    )(depth_id, surface, tables)
+    wave = lax.all_to_all(packed, "lat", 0, 0, tiled=True)
+    listed = wave[:, rows - tile_rows:, TILE:].reshape(entries, TILE).astype(jnp.int32)
+    listed = jnp.stack([listed[:, :HALF], listed[:, HALF:]], 0)
+    live_count = listed[:, :, 2 * slots]
+    index = listed[:, :, slots:2 * slots] * entries + listed[:, :, :slots]
+    live = jnp.arange(slots)[None, None, :] < live_count[:, :, None]
+    index = jnp.where(live, index, blocks * entries)
+    scale = 1.0 / jnp.sqrt(live_count.astype(jnp.float32))
+    own_freq = 2 * depth_id
+    half_freq = jnp.ones((1,), jnp.int32)
+    image = jnp.zeros((levels * entries, TILE), jnp.float32)
+    image = run_levels(
+        shots_own, 0, index, scale, wave, pool, remote_own, image, depth_id, own_freq
+    )
+    image = run_levels(
+        shots_half, tile_rows * shots_own, index, scale, wave, pool, remote_half, image, depth_id,
+        half_freq,
+    )
+    freq_size = lax.axis_size("freq")
+    spread = jnp.broadcast_to(
+        image.reshape(levels, lat_size, 1, tile_rows, TILE),
+        (levels, lat_size, freq_size, tile_rows, TILE),
+    ).reshape(levels * lat_size * freq_size, tile_rows, TILE)
+    parts = lax.all_to_all(spread, ("depth", "lat", "freq"), 0, 0, tiled=True)
+    summed = jnp.sum(parts, axis=0).reshape(1, lateral_width)
+    passing = 1.0 - refl
+    factor = jnp.where(depth_index == levels - 1, passing * passing, 1.0)
+    return summed * factor / (freqs_here * freq_size * shot_total)
+
+
+def fits_fast(mesh, surface, pool, tile_ids):
+    depth, lat, freq = (mesh.shape[name] for name in ("depth", "lat", "freq"))
+    freqs, _, shots, width = surface.shape
+    return (
+        depth == 2
+        and pool.shape[0] == depth
+        and freqs == 3 * freq
+        and shots == 16 * lat
+        and tile_ids.shape[1] * TILE == width
+        and tile_ids.shape[1] == 8 * lat
+        and 2 * tile_ids.shape[2] < HALF
+        and max(tile_ids.shape[1], pool.shape[2]) <= 256
+    )
+
+
 def solution(mesh):
     placed = (
         P("freq", None, None, "lat"),
@@ -96,6 +349,13 @@
         P("depth", "lat", None),
         P("depth", "lat"),
     )
-    return jax.shard_map(
-        per_device, mesh=mesh, in_specs=placed, out_specs=P("depth", "lat"), check_vma=False
-    )
+
+    def whole(surface, refl, pool, tile_ids, block_ids, counts):
+        fast = fits_fast(mesh, surface, pool, tile_ids)
+        mapped = jax.shard_map(
+            per_device_fast if fast else per_device, mesh=mesh, in_specs=placed,
+            out_specs=P("depth", "lat"), check_vma=False,
+        )
+        return mapped(surface, refl, pool, tile_ids, block_ids, counts)
+
+    return whole

time: 194 us -> 75.5 us (0.39)
  waiting for transfers between devices: 73.6 us -> 26.6 us
  local copies, waits for them, and re-layouts: 39.5 us -> 5.7 us
  Pallas kernels: 0 us -> 23.1 us
  blocking collectives: 26.7 us -> 5.41 us
  matrix products: 20.5 us -> 0 us
  between operations: 13.4 us -> 0.1 us
  other arithmetic: 11.5 us -> 2.17 us
  starting transfers between devices: 8.71 us -> 11.9 us
    ppermute x4 -> x2, waiting for transfers between devices: 44.9 us -> 0.01 us  [the longest x1 0.01 us: per_device_fast(): remote_half = lax.ppermute(pool[0, 1], 'depth', swap)]
    gather x4 -> x0, local copies, waits for them, and re-layouts: 33.3 us -> none  [the longest x2 17 us: extrapolate(): jnp.take(tile_grid, local_ids, axis=3)]
    all_gather x1 -> x0, waiting for transfers between devices: 28 us -> none  [per_device(): pool_all = lax.all_gather(pool, 'depth', axis=0, tiled=True)]
    all_to_all x0 -> x2, waiting for transfers between devices: none -> 26.6 us  [the longest x1 18.4 us: per_device_fast(): wave = lax.all_to_all(packed, 'lat', 0, 0, tiled=True)]
    pallas_call x0 -> x3, Pallas kernels: none -> 23.1 us  [the longest x2 20.1 us: run_levels(): pl.pallas_call(functools.partial(level_kernel, shots, row_start, levels,...]
    dot_general x2 -> x0, matrix products: 20.5 us -> none  [extrapolate(): jnp.einsum('fsarkt,frktc->rfsac', picked, chosen, preferred_element_type=...]
    all_gather x4 -> x1, blocking collectives: 19.2 us -> 5.41 us  [per_device_fast(): tables = lax.all_gather(tables, 'depth', axis=0, tiled=True)]
    all_to_all x0 -> x2, starting transfers between devices: none -> 9.85 us  [the longest x1 6.34 us: per_device_fast(): wave = lax.all_to_all(packed, 'lat', 0, 0, tiled=True)]
  transfers between devices with their start and end apart: 5 -> 4, of which waited for: 3 -> 2; matrix products, arithmetic and copies ran while one was open for 11% -> 3% of each run, Pallas kernels for 0% -> 15%
where the time goes in v1:
time: 75.5 us; the launch traced here: 75 us
  waiting for transfers between devices  26.6 us (35%)
  Pallas kernels  23.1 us (31%)
  starting transfers between devices  11.9 us (16%)
  local copies, waits for them, and re-layouts  5.7 us (8%)
  blocking collectives  5.41 us (7%)
  other arithmetic  2.17 us (3%)
    pallas_call x2, Pallas kernels, run_levels(): pl.pallas_call(functools.partial(level_kernel, shots, row_start, levels,...  20.1 us
    all_to_all x1, waiting for transfers between devices, per_device_fast(): wave = lax.all_to_all(packed, 'lat', 0, 0, tiled=True)  18.4 us
    all_to_all x1, waiting for transfers between devices, per_device_fast(): parts = lax.all_to_all(spread, ('depth', 'lat', 'freq'), 0, 0, tiled=True)  8.2 us
    all_to_all x1, starting transfers between devices, per_device_fast(): wave = lax.all_to_all(packed, 'lat', 0, 0, tiled=True)  6.34 us
    all_gather x1, blocking collectives, per_device_fast(): tables = lax.all_gather(tables, 'depth', axis=0, tiled=True)  5.41 us
    all_to_all x1, starting transfers between devices, per_device_fast(): parts = lax.all_to_all(spread, ('depth', 'lat', 'freq'), 0, 0, tiled=True)  3.51 us
    pallas_call x1, Pallas kernels, per_device_fast(): pl.pallas_call(functools.partial(pack_kernel, lat_size), out_shape=jax.Sh...  2.96 us
    ppermute x1, starting transfers between devices, per_device_fast(): remote_own = lax.ppermute(theirs, 'depth', swap)  1.58 us
  transfers between devices with their start and end apart: 4, of which 2 were waited for; matrix products, arithmetic and copies ran while one was open for 3% of the time, Pallas kernels for 15%

profile of v1, /device:TPU:0, one launch (start us, length us, event | category | flops | bytes accessed | tf_op | source)
XLA Modules:
  0.0 75.0 jit_solution(7528747730052394207)
XLA Ops:
  0.0 0.7 copy.14
  0.7 0.8 %add_convert_fusion = f32[8,21]{1,0:T(8,128)S(1)} fusion(s32[8,1]{1,0:T(8,128)S(1)} %copy.14, s32[8,10]{1,0:T(8,128)} %bitcast.32, s32[8,10]{1,0:T(8,128)} %bitcast.33), kind=kLoop, calls=%fused_computation.13 | loop fusion | flops 504 | bytes 1344 | tf_op jit(solution)/shard_map/convert_element_type | solution.py:280
  1.5 0.7 select_maximum_fusion
  2.2 5.4 %all-gather = f32[32,128]{1,0:T(8,128)} all-gather(f32[16,128]{1,0:T(8,128)S(1)} %select_maximum_fusion), channel_id=2, replica_groups=mesh['depth'=2,'lat'=8,'freq'=2] {'depth'}, dimensions={0}, use_global_device_ids=true | all-gather | bytes 24576 | tf_op jit(solution)/shard_map/all_gather | solution.py:283
  7.6 3.0 %pack.1 = bf16[8,208,256]{2,1,0:T(8,128)(2,1)} custom-call(s32[1]{0:T(128)} %bitcast.depth_ref, bf16[3,2,128,1024]{3,2,1,0:T(8,128)(2,1)} %surface_ref.1, f32[2,16,128]{2,1,0:T(8,128)} %bitcast.27), custom_call_target="tpu_custom_call" | custom-call | tf_op jit(solution)/shard_map/pack/pallas_call | solution.py:286
  10.6 6.3 %all-to-all-start = ((bf16[8,208,256]{2,1,0:T(8,128)(2,1)}), bf16[8,208,256]{2,1,0:T(8,128)(2,1)S(1)}, u32[]{:S(2)}, u32[]{:S(2)}) async-start(bf16[8,208,256]{2,1,0:T(8,128)(2,1)} %pack.1), calls=%async_computation | async-start | bytes 1703936 | tf_op jit(solution)/shard_map/all_to_all | solution.py:298
  16.9 0.0 copy-done.1
  16.9 0.1 dynamic-slice_bitcast_fusion
  17.0 1.6 %collective-permute-start.1 = (bf16[8,128,256]{2,1,0:T(8,128)(2,1)S(1)}, bf16[8,128,256]{2,1,0:T(8,128)(2,1)S(1)}, u32[]{:S(2)}, u32[]{:S(2)}) collective-permute-start(bf16[8,128,256]{2,1,0:T(8,128)(2,1)S(1)} %get-tuple-element.7), channel_id=1, source_target_pairs={{0,16},{16,0},{1,17},{17,1},{2,18},{18,2},{3,19},{19,3},{4,20},{20... | collective-permute-start | bytes 1572872 | tf_op jit(solution)/shard_map/ppermute | solution.py:278
  18.6 0.5 collective-permute-start
  19.1 18.4 %all-to-all-done.wave_ref = bf16[8,208,256]{2,1,0:T(8,128)(2,1)S(1)} async-done(((bf16[8,208,256]{2,1,0:T(8,128)(2,1)}), bf16[8,208,256]{2,1,0:T(8,128)(2,1)S(1)}, u32[]{:S(2)}, u32[]{:S(2)}) %all-to-all-start) | async-done | bytes 852000 | tf_op jit(solution)/shard_map/all_to_all | solution.py:298
  37.5 0.1 fusion.4
  37.6 0.1 copy.18
  37.7 0.1 copy.19
  37.8 0.1 copy.17
  37.9 0.7 reshape.30.index_ref
  38.6 0.7 sqrt.6.scale_ref
  39.3 0.0 collective-permute-done.1.remote_ref
  39.3 0.7 broadcast_in_dim.22.image_in_ref
  40.0 0.0 copy-done
  40.0 0.2 copy-done.4
  40.2 11.2 %levels_16.1.image_in_ref = f32[128,128]{1,0:T(8,128)} custom-call(s32[1280]{0:T(1024)} %reshape.30.index_ref, f32[128]{0:T(128)} %sqrt.6.scale_ref, bf16[8,208,256]{2,1,0:T(8,128)(2,1)} %copy-done, bf16[1,3,8,128,256]{4,3,2,1,0:T(8,128)(2,1)} %local_ref.3, bf16[8,128,256]{2,1,0:T(8,128)(2,1)} %copy-done.4, f32[128,128]{1,0:T(8,128)} %broadcast_in_dim.22.image_in_ref, ...), custom_call_target="tpu_custom_call" | custom-call | flops 2147483648 | bytes 2097152 | tf_op jit(solution)/shard_map/levels_16/pallas_call | solution.py:244
  51.3 0.0 copy-start.2
  51.3 0.0 collective-permute-done.remote_ref
  51.4 0.0 copy-start.3
  51.4 0.8 %copy-done.3 = bf16[8,128,256]{2,1,0:T(8,128)(2,1)} copy-done((bf16[8,128,256]{2,1,0:T(8,128)(2,1)}, bf16[8,128,256]{2,1,0:T(8,128)(2,1)S(1)}, u32[]{:S(2)}) %copy-start.3) | copy-done | bytes 524312
  52.2 8.9 %levels_8.1 = f32[128,128]{1,0:T(8,128)} custom-call(s32[1280]{0:T(1024)} %reshape.30.index_ref, f32[128]{0:T(128)} %sqrt.6.scale_ref, bf16[8,208,256]{2,1,0:T(8,128)(2,1)} %copy-done, bf16[1,3,8,128,256]{4,3,2,1,0:T(8,128)(2,1)} %local_ref.3, bf16[8,128,256]{2,1,0:T(8,128)(2,1)} %copy-done.3, f32[128,128]{1,0:T(8,128)} %levels_16.1.image_in_ref, ...), custom_call_target="tpu_custom_call" | custom-call | flops 1073741824 | bytes 1572864 | tf_op jit(solution)/shard_map/levels_8/pallas_call | solution.py:244
  61.1 1.5 %broadcast_in_dim.24 = f32[2,8,2,8,128]{4,3,2,1,0:T(8,128)} broadcast(f32[2,8,8,128]{3,2,1,0:T(8,128)} %bitcast.28), dimensions={0,1,3,4} | broadcast | bytes 196608 | tf_op jit(solution)/shard_map/broadcast_in_dim | solution.py:317
  62.6 3.5 %all-to-all-start.1 = ((f32[32,8,128]{2,1,0:T(8,128)}), f32[32,8,128]{2,1,0:T(8,128)S(1)}, u32[]{:S(2)}, u32[]{:S(2)}) async-start(f32[32,8,128]{2,1,0:T(8,128)} %bitcast.13), calls=%async_computation.1 | async-start | bytes 262144 | tf_op jit(solution)/shard_map/all_to_all | solution.py:321
  66.1 8.2 %all-to-all-done.1 = f32[32,8,128]{2,1,0:T(8,128)S(1)} async-done(((f32[32,8,128]{2,1,0:T(8,128)}), f32[32,8,128]{2,1,0:T(8,128)S(1)}, u32[]{:S(2)}, u32[]{:S(2)}) %all-to-all-start.1) | async-done | bytes 131104 | tf_op jit(solution)/shard_map/all_to_all | solution.py:321
  74.4 0.0 copy-done.2
  74.4 0.6 fusion.3
  (7 shorter events, 0.1 us)
Async XLA Ops:
  7.6 9.3 %copy-start.1 = (bf16[1,3,8,128,256]{4,3,2,1,0:T(8,128)(2,1)S(1)}, bf16[1,3,8,128,256]{4,3,2,1,0:T(8,128)(2,1)}, u32[]{:S(2)}) copy-start(bf16[1,3,8,128,256]{4,3,2,1,0:T(8,128)(2,1)} %local_ref.3) | copy-start | bytes 4718596
  10.6 26.9 %all-to-all-start = ((bf16[8,208,256]{2,1,0:T(8,128)(2,1)}), bf16[8,208,256]{2,1,0:T(8,128)(2,1)S(1)}, u32[]{:S(2)}, u32[]{:S(2)}) async-start(bf16[8,208,256]{2,1,0:T(8,128)(2,1)} %pack.1), calls=%async_computation | async-start | bytes 1703936 | tf_op jit(solution)/shard_map/all_to_all | solution.py:298
  17.0 22.3 %collective-permute-start.1 = (bf16[8,128,256]{2,1,0:T(8,128)(2,1)S(1)}, bf16[8,128,256]{2,1,0:T(8,128)(2,1)S(1)}, u32[]{:S(2)}, u32[]{:S(2)}) collective-permute-start(bf16[8,128,256]{2,1,0:T(8,128)(2,1)S(1)} %get-tuple-element.7), channel_id=1, source_target_pairs={{0,16},{16,0},{1,17},{17,1},{2,18},{18,2},{3,19},{19,3},{4,20},{20... | collective-permute-start | bytes 1572872 | tf_op jit(solution)/shard_map/ppermute | solution.py:278
  18.6 32.7 %collective-permute-start = (bf16[8,128,256]{2,1,0:T(8,128)(2,1)S(1)}, bf16[8,128,256]{2,1,0:T(8,128)(2,1)S(1)}, u32[]{:S(2)}, u32[]{:S(2)}) collective-permute-start(bf16[8,128,256]{2,1,0:T(8,128)(2,1)S(1)} %get-tuple-element.8), channel_id=1, source_target_pairs={{0,16},{16,0},{1,17},{17,1},{2,18},{18,2},{3,19},{19,3},{4,20},{20... | collective-permute-start | bytes 1572872 | tf_op jit(solution)/shard_map/ppermute | solution.py:279
  37.5 2.5 %copy-start = (bf16[8,208,256]{2,1,0:T(8,128)(2,1)}, bf16[8,208,256]{2,1,0:T(8,128)(2,1)S(1)}, u32[]{:S(2)}) copy-start(bf16[8,208,256]{2,1,0:T(8,128)(2,1)S(1)} %all-to-all-done.wave_ref) | copy-start | bytes 2555908
  39.3 0.9 %copy-start.4 = (bf16[8,128,256]{2,1,0:T(8,128)(2,1)}, bf16[8,128,256]{2,1,0:T(8,128)(2,1)S(1)}, u32[]{:S(2)}) copy-start(bf16[8,128,256]{2,1,0:T(8,128)(2,1)S(1)} %collective-permute-done.1.remote_ref) | copy-start | bytes 1572868
  51.3 23.0 %copy-start.2 = (f32[1,1024]{1,0:T(1,128)S(1)}, f32[1,1024]{1,0:T(1,128)}, u32[]{:S(2)}) copy-start(f32[1,1024]{1,0:T(1,128)} %param.7) | copy-start | bytes 12292
  51.4 0.8 %copy-start.3 = (bf16[8,128,256]{2,1,0:T(8,128)(2,1)}, bf16[8,128,256]{2,1,0:T(8,128)(2,1)S(1)}, u32[]{:S(2)}) copy-start(bf16[8,128,256]{2,1,0:T(8,128)(2,1)S(1)} %collective-permute-done.remote_ref) | copy-start | bytes 1572868
  62.6 11.7 %all-to-all-start.1 = ((f32[32,8,128]{2,1,0:T(8,128)}), f32[32,8,128]{2,1,0:T(8,128)S(1)}, u32[]{:S(2)}, u32[]{:S(2)}) async-start(f32[32,8,128]{2,1,0:T(8,128)} %bitcast.13), calls=%async_computation.1 | async-start | bytes 262144 | tf_op jit(solution)/shard_map/all_to_all | solution.py:321
